TPU v7x, 32 devices: a whole 2x2x4 slice. The times are simulated.
32 devices in a mesh: parts: 2 (over y), req: 4 (over z), tp: 2 (over x), sp: 2 (over core).
Axes of the slice: x: 2, y: 2, z: 4, core: 2. Of those that a mesh axis runs over, the one named last changes fastest.
Arguments:
- prompt_x: bfloat16 [1024, 16384], P(('parts', 'req', 'sp'), 'tp'), parts along dimension 0, may hold values from -600 to 600
- prompt_b: bfloat16 [1024, 8, 128], P(('parts', 'req', 'sp'), 'tp'), parts along dimension 0, may hold values from -0.5 to 0.5
- prompt_dt: float32 [1024, 256], P(('parts', 'req', 'sp'), 'tp'), parts along dimension 0, may hold values from 0.5 to 2
- cont_x: bfloat16 [8, 256, 16384], P(('parts', 'req'), 'sp', 'tp'), parts along dimension 0, may hold values from -6 to 6
- cont_bc: bfloat16 [8, 256, 2, 8, 128], P(('parts', 'req'), 'sp', None, 'tp'), parts along dimension 0, may hold values from -0.5 to 0.5
- cont_dt: float32 [8, 256, 256], P(('parts', 'req'), 'sp', 'tp'), parts along dimension 0, may hold values from 0.5 to 2
- decay_rate: float32 [256], P('tp'), may hold values from 0.0063476562 to 0.05
- skip_gain: float32 [256], P('tp'), may hold values from 0.5 to 1.5
- norm_gain: float32 [16384], P('tp'), may hold values from 0.25 to 1.75
- steer_vecs: float32 [7, 16384], P(None, 'tp'), may hold values from -3 to 3
- mult_table: float32 [9], replicated, may hold values from -3 to 3
- mult_idx: int32 [8], P(('parts', 'req')), parts along dimension 0, may hold values from 0 to 8
- behav_idx: int32 [8], P(('parts', 'req')), parts along dimension 0, may hold values from 0 to 6
Outputs:
- steered_out: bfloat16 [8, 256, 16384], P(('parts', 'req'), 'sp', 'tp'), parts along dimension 0
There are 2 independent parts, one for each index of `parts`. A program takes and returns all parts, laid end to end along the dimension named above; an argument that names none is the same for every part. Nothing has to cross between parts.
All inputs are finite; a program needn't handle non-finite values.
Results may differ from a plain program's by a relative error of at most 0.008.
Values sent between devices are 32-bit elements; how exact they have to be, the bound alone decides.
A program may use at most 320 MiB of HBM per device.

v0:
```python
import jax
import jax.numpy as jnp
from jax import lax
from jax.sharding import PartitionSpec as P

HEADS = 256
HEAD_DIM = 64


def block_state(rows_x, rows_b, rows_dt, decay_rate, groups):
    length = rows_x.shape[0]
    head_count = decay_rate.shape[0]
    per_group = head_count // groups
    head_size = rows_x.shape[1] // head_count
    cumulative = jnp.cumsum(-decay_rate[None, :] * rows_dt, axis=0)
    block_total = cumulative[-1]
    weight = jnp.exp(block_total[None, :] - cumulative) * rows_dt
    scaled = (
        rows_x.astype(jnp.float32).reshape(length, head_count, head_size) * weight[:, :, None]
    ).astype(jnp.bfloat16)
    scaled = scaled.reshape(length, groups, per_group, head_size)
    local_state = jnp.einsum("tgqp,tgn->gqpn", scaled, rows_b, preferred_element_type=jnp.float32)
    carried = jnp.einsum(
        "tgq,tgn->gqn",
        weight.reshape(length, groups, per_group),
        rows_b.astype(jnp.float32),
        precision=lax.Precision.HIGHEST,
    )
    return (
        block_total,
        local_state.reshape(head_count, head_size, -1),
        carried.reshape(head_count, -1),
        cumulative,
    )


def intra_block(steered, bmat, cmat, rows_dt, cumulative, groups):
    length = steered.shape[0]
    head_count = rows_dt.shape[1]
    per_group = head_count // groups
    head_size = steered.shape[1] // head_count
    products = jnp.einsum("tgn,sgn->gts", cmat, bmat, preferred_element_type=jnp.float32)
    lower_mask = lax.broadcasted_iota(jnp.int32, (length, length), 0) >= lax.broadcasted_iota(
        jnp.int32, (length, length), 1
    )
    row_factor = jnp.exp(cumulative).reshape(length, groups, per_group).transpose(1, 2, 0)
    col_factor = (
        (jnp.exp(-cumulative) * rows_dt).reshape(length, groups, per_group).transpose(1, 2, 0)
    )
    full = products[:, None, :, :] * row_factor[:, :, :, None] * col_factor[:, :, None, :]
    mixing = jnp.where(lower_mask[None, None], full, 0.0).astype(jnp.bfloat16)
    input_groups = steered.reshape(length, groups, per_group, head_size)
    outputs = jnp.einsum(
        "gqts,sgqp->tgqp", mixing, input_groups, preferred_element_type=jnp.float32
    )
    return outputs.reshape(length, head_count, head_size)


def local(
    prompt_x,
    prompt_b,
    prompt_dt,
    cont_x,
    cont_bc,
    cont_dt,
    decay_rate,
    skip_gain,
    norm_gain,
    steer_vecs,
    mult_table,
    mult_idx,
    behav_idx,
):
    groups = prompt_b.shape[1]
    head_count = decay_rate.shape[0]
    per_group = head_count // groups
    head_size = norm_gain.shape[0] // head_count
    prompt_total, prompt_state, prompt_carry, unused = block_state(
        prompt_x, prompt_b, prompt_dt, decay_rate, groups
    )
    place = lax.axis_index(("req", "sp"))
    totals = lax.all_gather(prompt_total, ("req", "sp"))
    later = lax.broadcasted_iota(jnp.int32, totals.shape, 0) > place
    remaining = jnp.exp(jnp.sum(jnp.where(later, totals, 0.0), axis=0))
    prefix_state, prefix_carry = lax.psum(
        (remaining[:, None, None] * prompt_state, remaining[:, None] * prompt_carry), ("req", "sp")
    )
    picked = lax.broadcasted_iota(jnp.int32, mult_table.shape, 0) == mult_idx[0]
    multiplier = jnp.sum(jnp.where(picked, mult_table, 0.0))
    choose = lax.broadcasted_iota(jnp.int32, (steer_vecs.shape[0], 1), 0) == behav_idx[0]
    vector = jnp.sum(jnp.where(choose, steer_vecs, 0.0), axis=0)
    steered = (cont_x[0].astype(jnp.float32) + multiplier * vector[None, :]).astype(jnp.bfloat16)
    bmat = cont_bc[0, :, 0]
    cmat = cont_bc[0, :, 1]
    rows_dt = cont_dt[0]
    length = steered.shape[0]
    block_total, local_state, carried, cumulative = block_state(
        steered, bmat, rows_dt, decay_rate, groups
    )
    before_total, before_state = lax.ppermute((block_total, local_state), "sp", [(0, 1)])
    inner = intra_block(steered, bmat, cmat, rows_dt, cumulative, groups)
    start_state = (
        prefix_state
        + multiplier * vector.reshape(head_count, head_size)[:, :, None] * prefix_carry[:, None, :]
    )
    incoming = jnp.exp(before_total)[:, None, None] * start_state + before_state
    incoming_round = incoming.astype(jnp.bfloat16).reshape(groups, per_group, head_size, -1)
    from_state = jnp.einsum(
        "tgn,gqpn->tgqp", cmat, incoming_round, preferred_element_type=jnp.float32
    ).reshape(length, head_count, head_size)
    skipped = skip_gain[None, :, None] * steered.astype(jnp.float32).reshape(
        length, head_count, head_size
    )
    mixed = (inner + jnp.exp(cumulative)[:, :, None] * from_state + skipped).reshape(
        length, head_count * head_size
    )
    squares = jnp.sum(mixed * mixed, axis=1)
    total_squares = lax.psum(squares, "tp")
    meansq = total_squares / (HEADS * HEAD_DIM)
    return (mixed * lax.rsqrt(meansq + 1e-05)[:, None] * norm_gain[None, :]).astype(jnp.bfloat16)[
        None
    ]


def solution(mesh):
    return jax.shard_map(
        local,
        mesh=mesh,
        in_specs=(
            P(("parts", "req", "sp"), "tp"),
            P(("parts", "req", "sp"), "tp", None),
            P(("parts", "req", "sp"), "tp"),
            P(("parts", "req"), "sp", "tp"),
            P(("parts", "req"), "sp", None, "tp", None),
            P(("parts", "req"), "sp", "tp"),
            P("tp"),
            P("tp"),
            P("tp"),
            P(None, "tp"),
            P(),
            P(("parts", "req")),
            P(("parts", "req")),
        ),
        out_specs=P(("parts", "req"), "sp", "tp"),
        check_vma=False,
    )
```

profile of v0, /device:TPU:0, one launch (start us, length us, event | category | flops | bytes accessed | tf_op | source)
XLA Modules:
  0.0 185.2 jit_solution(16064497047261371977)
XLA Ops:
  6.5 0.7 neg.9
  7.2 0.8 bitcast_multiply_fusion.4
  8.3 0.7 copy.42
  9.0 1.6 copy.43
  11.9 1.1 select_reduce_fusion
  13.1 1.3 fusion.34
  14.3 0.6 broadcast_multiply_fusion.1
  15.1 0.5 copy-done.5
  15.6 3.2 %copy.39 = bf16[1,128,8192]{1,2,0:T(8,128)(2,1)S(1)} copy(bf16[1,128,8192]{2,1,0:T(8,128)(2,1)} %param.16) | data formatting | bytes 4194304 | tf_op args[3]
  18.8 1.2 fusion.36
  20.0 1.6 fusion.37
  21.6 2.8 %fusion.17 = f32[4,32,64,128]{3,2,1,0:T(8,128)} fusion(f32[128,4,32]{0,2,1:T(8,128)S(1)} %get-tuple-element.14, bf16[1,128,1,4,128]{4,3,2,1,0:T(4,128)(2,1)S(1)} %get-tuple-element.8, f32[4,32,64]{2,1,0:T(8,128)S(1)} %mul.204, bf16[128,4,32,64]{0,3,2,1:T(8,128)(2,1)S(1)} %bitcast.77), kind=kOutput, calls=%fused_computation.27 | convolution fusion | flops 274726912 | bytes 6520832 | tf_op jit(solution)/shard_map/tgqp,tgn->gqpn/dot_general | solution.py:22
  24.3 4.3 %collective-permute-start.1 = (f32[128,64,128]{2,1,0:T(8,128)}, f32[128,64,128]{2,1,0:T(8,128)}, u32[]{:S(2)}, u32[]{:S(2)}) collective-permute-start(f32[128,64,128]{2,1,0:T(8,128)} %bitcast.24), channel_id=1, source_target_pairs={{0,1},{2,3},{4,5},{6,7},{8,9},{10,11},{12,13},{14,15},{16,17},{18,... | collective-permute-start | bytes 12582920 | tf_op jit(solution)/shard_map/ppermute | solution.py:100
  28.7 0.6 broadcast_multiply_fusion
  29.3 1.4 reduce_window_sum.26
  30.7 0.7 slice_bitcast_fusion.1
  31.4 1.4 exponential_multiply_fusion.1
  32.8 1.5 copy.45
  34.2 2.4 %copy.53 = f32[64,8192]{0,1:T(8,128)} copy(bf16[64,8192]{1,0:T(8,128)(2,1)S(1)} %copy-done.2) | data formatting | bytes 3145728 | tf_op jit(solution)/shard_map/reshape | solution.py:19
  36.6 12.7 %all-gather = f32[8,1,128]{2,1,0:T(1,128)S(1)} all-gather(f32[1,1,128]{2,1,0:T(1,128)S(1)} %get-tuple-element.17), channel_id=1, replica_groups=mesh['parts'=2,'req'=4,'tp'=2,'sp'=2] {'req','sp'}, dimensions={0}, use_global_device_ids=true | all-gather | bytes 4608 | tf_op jit(solution)/shard_map/all_gather | solution.py:82
  49.5 1.0 fusion.32
  50.5 0.7 bitcast_multiply_fusion.3
  51.2 2.9 %fusion.16 = f32[4,32,64,128]{3,2,1,0:T(8,128)S(1)} fusion(f32[64,4,32,64]{0,3,2,1:T(8,128)} %bitcast.80, f32[64,4,32]{0,2,1:T(8,128)} %bitcast.85, bf16[64,4,128,1]{2,1,0,3:T(4,128)(2,1)S(1)} %bitcast.76), kind=kOutput, calls=%fused_computation.26 | convolution fusion | flops 135266304 | bytes 6389760 | tf_op jit(solution)/shard_map/tgqp,tgn->gqpn/dot_general | solution.py:22
  54.1 2.3 %bitcast_multiply_fusion.1 = f32[128,64,128]{2,1,0:T(8,128)} fusion(f32[4,32,64,128]{3,2,1,0:T(8,128)S(1)} %fusion.16, f32[128]{0:T(128)S(1)} %exp.44), kind=kLoop, calls=%fused_computation.10 | loop fusion | flops 1048576 | bytes 8389120 | tf_op jit(solution)/shard_map/mul | solution.py:86
  56.4 2.3 %collective-permute-start = (f32[128]{0:T(128)S(1)}, f32[128]{0:T(128)S(1)}, u32[]{:S(2)}, u32[]{:S(2)}) collective-permute-start(f32[128]{0:T(128)S(1)} %get-tuple-element.15), channel_id=1, source_target_pairs={{0,1},{2,3},{4,5},{6,7},{8,9},{10,11},{12,13},{14,15},{16,17},{18,... | collective-permute-start | bytes 1544 | tf_op jit(solution)/shard_map/ppermute | solution.py:100
  59.0 6.3 %fusion.4 = f32[4,32,64,128]{3,2,1,0:T(8,128)} fusion(f32[4,32,128]{2,1,0:T(8,128)S(1)} %copy-done.10, f32[4,32,128]{2,1,0:T(8,128)S(1)} %copy-done.9, f32[4,128,128]{2,1,0:T(8,128)S(1)} %fusion.24, pred[128,128]{1,0:T(8,128)(4,1)S(1)} %iota_compare_fusion, f32[4,32,64]{2,1,0:T(8,128)S(1)} %mul.204, bf16[128,4,32,64]{0,3,2,1:T(8,128)(2,1)S(1)} %bitcast.78), kind=kOutput, calls=%fused_computation.7 | convolution fusion | flops 279969792 | bytes 6733824 | tf_op jit(solution)/shard_map/gqts,sgqp->tgqp/dot_general | solution.py:53
  65.8 87.1 %all-reduce.3.cloned.1.call-done = (f32[128,64,128]{2,1,0:T(8,128)}, f32[128,128]{1,0:T(8,128)}) async-done(((f32[128,64,128]{2,1,0:T(8,128)}, f32[128,128]{1,0:T(8,128)}), (f32[128,64,128]{2,1,0:T(8,128)}, f32[128,128]{1,0:T(8,128)})) %all-reduce.3.cloned.1.call-update) | async-done | bytes 4259856 | tf_op jit(solution)/shard_map/psum | solution.py:85
  152.9 4.4 %add_convert_fusion.1 = bf16[128,64,128]{2,1,0:T(8,128)(2,1)S(1)} fusion(f32[128,64,128]{2,1,0:T(8,128)} %collective-permute-done.1, f32[128,64,128]{2,1,0:T(8,128)} %get-tuple-element.5, f32[128,128]{1,0:T(8,128)} %get-tuple-element.6, f32[128,64]{1,0:T(8,128)S(1)} %mul.225, f32[128]{0:T(128)S(1)} %exp.43), kind=kLoop, calls=%fused_computation.18 | loop fusion | flops 5242880 | bytes 10584576 | tf_op jit(solution)/shard_map/convert_element_type | solution.py:107
  157.6 3.2 %fusion.3 = (f32[128]{0:T(128)S(1)}, f32[4,32,64,128]{3,2,1,0:T(8,128)}) fusion(f32[4,32,64,128]{3,2,1,0:T(8,128)S(1)} %copy-done.1, f32[4,32]{1,0:T(4,128)S(1)} %mul.242, f32[128,4,32]{0,2,1:T(8,128)S(1)} %copy-done.7, bf16[4,32,64,128]{3,2,1,0:T(8,128)(2,1)S(1)} %bitcast.83, bf16[1,128,1,4,128]{4,3,2,1,0:T(4,128)(2,1)S(1)} %get-tuple-element.7, ...), kind=kOutput, calls=%fused_computation.6 | convolution fusion | flops 278921088 | bytes 12813312 | tf_op jit(solution)/shard_map/tgn,gqpn->tgqp/dot_general | solution.py:108
  160.8 4.9 %psum.23 = f32[128]{0:T(128)S(1)} all-reduce(f32[128]{0:T(128)S(1)} %get-tuple-element.19), channel_id=1, replica_groups=mesh['parts'=2,'req'=4,'tp'=2,'sp'=2] {'tp'}, use_global_device_ids=true, to_apply=%region_8.9 | all-reduce | flops 128 | bytes 1024 | tf_op jit(solution)/shard_map/psum | solution.py:118
  165.7 8.5 %fusion.10 = bf16[1,128,8192]{1,2,0:T(8,128)(2,1)} fusion(f32[1,128,8192]{1,2,0:T(8,128)} %bitcast.81, f32[1,128,8192]{1,2,0:T(8,128)} %bitcast.82, f32[8192]{0:T(1024)S(1)} %copy-done.11, f32[128]{0:T(128)S(1)} %add_rsqrt_fusion, f32[8192]{0:T(1024)S(1)} %copy-done.6, f32[8192]{0:T(1024)S(1)} %mul.237, f32[128,128]{0,1:T(8,128)S(1)} %copy.44, ...), kind=kLoop, calls=%fused_computation.16 | loop fusion | flops 11534336 | bytes 12747264 | tf_op jit(solution)/shard_map/convert_element_type | solution.py:120
  174.3 4.1 %copy.49 = bf16[1,128,8192]{2,1,0:T(8,128)(2,1)} copy(bf16[1,128,8192]{1,2,0:T(8,128)(2,1)} %fusion.10) | data formatting | bytes 4194304 | tf_op jit(solution)/shard_map/convert_element_type | solution.py:120
  (47 shorter events, 1.4 us)
Async XLA Ops:
  6.5 42.9 %copy-start = (bf16[64,4,128]{2,1,0:T(4,128)(2,1)S(1)}, bf16[64,4,128]{2,1,0:T(4,128)(2,1)}, u32[]{:S(2)}) copy-start(bf16[64,4,128]{2,1,0:T(4,128)(2,1)} %param.14) | copy-start | bytes 196612
  6.5 146.3 %all-reduce.3.cloned.1.call-start = ((), (), s32[]{:S(2)}) async-start(), calls=%async_computation | async-start | bytes 8519680 | tf_op jit(solution)/shard_map/psum | solution.py:85
  8.2 6.7 %copy-start.3 = (f32[128,128]{1,0:T(8,128)}, f32[128,128]{1,0:T(8,128)S(1)}, u32[]{:S(2)}) copy-start(f32[128,128]{1,0:T(8,128)S(1)} %reduce_window_sum.24) | copy-start | bytes 196612
  15.0 0.6 copy-start.5
  18.8 9.8 %copy-start.8 = (f32[64,128]{1,0:T(8,128)S(1)}, f32[64,128]{1,0:T(8,128)}, u32[]{:S(2)}) copy-start(f32[64,128]{1,0:T(8,128)} %param.15) | copy-start | bytes 98308
  18.8 15.4 %copy-start.2 = (bf16[64,8192]{1,0:T(8,128)(2,1)S(1)}, bf16[64,8192]{1,0:T(8,128)(2,1)}, u32[]{:S(2)}) copy-start(bf16[64,8192]{1,0:T(8,128)(2,1)} %param.13) | copy-start | bytes 3145732
  24.3 128.5 %collective-permute-start.1 = (f32[128,64,128]{2,1,0:T(8,128)}, f32[128,64,128]{2,1,0:T(8,128)}, u32[]{:S(2)}, u32[]{:S(2)}) collective-permute-start(f32[128,64,128]{2,1,0:T(8,128)} %bitcast.24), channel_id=1, source_target_pairs={{0,1},{2,3},{4,5},{6,7},{8,9},{10,11},{12,13},{14,15},{16,17},{18,... | collective-permute-start | bytes 12582920 | tf_op jit(solution)/shard_map/ppermute | solution.py:100
  56.3 2.6 %copy-start.9 = (f32[4,32,128]{2,1,0:T(8,128)S(1)}, f32[4,32,128]{2,1,0:T(8,128)}, u32[]{:S(2)}) copy-start(f32[4,32,128]{2,1,0:T(8,128)} %get-tuple-element.12) | copy-start | bytes 196612
  56.3 2.6 %copy-start.10 = (f32[4,32,128]{2,1,0:T(8,128)S(1)}, f32[4,32,128]{2,1,0:T(8,128)}, u32[]{:S(2)}) copy-start(f32[4,32,128]{2,1,0:T(8,128)} %get-tuple-element.13) | copy-start | bytes 196612
  56.4 9.4 %collective-permute-start = (f32[128]{0:T(128)S(1)}, f32[128]{0:T(128)S(1)}, u32[]{:S(2)}, u32[]{:S(2)}) collective-permute-start(f32[128]{0:T(128)S(1)} %get-tuple-element.15), channel_id=1, source_target_pairs={{0,1},{2,3},{4,5},{6,7},{8,9},{10,11},{12,13},{14,15},{16,17},{18,... | collective-permute-start | bytes 1544 | tf_op jit(solution)/shard_map/ppermute | solution.py:100
  59.0 6.3 %copy-start.6 = (f32[8192]{0:T(1024)S(1)}, f32[8192]{0:T(1024)}, u32[]{:S(2)}) copy-start(f32[8192]{0:T(1024)} %copy-done.5) | copy-start | bytes 98308
  59.0 6.4 %copy-start.4 = (f32[128,128]{1,0:T(8,128)S(1)}, f32[128,128]{1,0:T(8,128)}, u32[]{:S(2)}) copy-start(f32[128,128]{1,0:T(8,128)} %copy-done.3) | copy-start | bytes 196612
  59.0 6.4 %copy-start.12 = (f32[128]{0:T(128)S(1)}, f32[128]{0:T(128)}, u32[]{:S(2)}) copy-start(f32[128]{0:T(128)} %param.20) | copy-start | bytes 1540
  152.9 4.7 %copy-start.1 = (f32[4,32,64,128]{3,2,1,0:T(8,128)S(1)}, f32[4,32,64,128]{3,2,1,0:T(8,128)}, u32[]{:S(2)}) copy-start(f32[4,32,64,128]{3,2,1,0:T(8,128)} %fusion.4) | copy-start | bytes 12582916
  152.9 4.7 %copy-start.7 = (f32[128,4,32]{0,2,1:T(8,128)S(1)}, f32[128,4,32]{0,2,1:T(8,128)}, u32[]{:S(2)}) copy-start(f32[128,4,32]{0,2,1:T(8,128)} %get-tuple-element.11) | copy-start | bytes 196612
  157.6 8.2 %copy-start.11 = (f32[8192]{0:T(1024)S(1)}, f32[8192]{0:T(1024)}, u32[]{:S(2)}) copy-start(f32[8192]{0:T(1024)} %param.21) | copy-start | bytes 98308
Sparse Core Ops, SparseCore 0:
  56.5 96.3 all-reduce.2
where the time goes:
time: 186 us; the launch traced here: 185 us
  waiting for transfers between devices  87.1 us (47%)
  other arithmetic  25.8 us (14%)
  blocking collectives  17.7 us (10%)
  local copies, waits for them, and re-layouts  16.7 us (9%)
  matrix products  16.4 us (9%)
  between operations  14.9 us (8%)
  starting transfers between devices  6.66 us (4%)
    psum x1, waiting for transfers between devices, local(): lax.psum((remaining[:, None, None] * prompt_state, remaining[:, None] * p...  87.1 us
    all_gather x1, blocking collectives, local(): totals = lax.all_gather(prompt_total, ('req', 'sp'))  12.7 us
    convert_element_type x1, other arithmetic, local(): (mixed * lax.rsqrt(meansq + 1e-05)[:, None] * norm_gain[None, :]).astype(...  8.54 us
    ppermute x2, starting transfers between devices, local(): lax.ppermute((block_total, local_state), 'sp', [(0, 1)])  6.66 us
    dot_general x1, matrix products, intra_block(): jnp.einsum('gqts,sgqp->tgqp', mixing, input_groups, preferred_element_typ...  6.31 us
    unnamed x29, local copies, waits for them, and re-layouts  6.24 us
    dot_general x2, matrix products, block_state(): jnp.einsum('tgqp,tgn->gqpn', scaled, rows_b, preferred_element_type=jnp.f...  5.64 us
    psum x1, blocking collectives, local(): total_squares = lax.psum(squares, 'tp')  4.92 us
  transfers between devices with their start and end apart: 3, of which 1 were waited for; matrix products, arithmetic and copies ran while one was open for 12% of the time, Pallas kernels for 0%

commit v1 on v0

--- a/solution.py
+++ b/solution.py
@@ -83,7 +83,10 @@
     later = lax.broadcasted_iota(jnp.int32, totals.shape, 0) > place
     remaining = jnp.exp(jnp.sum(jnp.where(later, totals, 0.0), axis=0))
     prefix_state, prefix_carry = lax.psum(
-        (remaining[:, None, None] * prompt_state, remaining[:, None] * prompt_carry), ("req", "sp")
+        lax.psum(
+            (remaining[:, None, None] * prompt_state, remaining[:, None] * prompt_carry), "sp"
+        ),
+        "req",
     )
     picked = lax.broadcasted_iota(jnp.int32, mult_table.shape, 0) == mult_idx[0]
     multiplier = jnp.sum(jnp.where(picked, mult_table, 0.0))

time: 186 us -> 253 us (1.36)
  waiting for transfers between devices: 87.1 us -> 166 us
  other arithmetic: 25.8 us -> 20.1 us
  local copies, waits for them, and re-layouts: 16.7 us -> 12.1 us
    psum x0 -> x1, waiting for transfers between devices: none -> 146 us  [local(): lax.psum(lax.psum((remaining[:, None, None] * prompt_state, remaining[:,...]
    psum x1, waiting for transfers between devices: 87.1 us -> 20 us  [local(): lax.psum((remaining[:, None, None] * prompt_state, remaining[:, None] * p...]
    unnamed x29 -> x19, local copies, waits for them, and re-layouts: 6.24 us -> 3.81 us
  transfers between devices with their start and end apart: 3 -> 4, of which waited for: 1 -> 2; matrix products, arithmetic and copies ran while one was open for 12% -> 6% of each run, Pallas kernels for 0% -> 0%
where the time goes in v1:
time: 253 us; the launch traced here: 252 us
  waiting for transfers between devices  166 us (66%)
  other arithmetic  20.1 us (8%)
  blocking collectives  18.3 us (7%)
  matrix products  15.6 us (6%)
  between operations  14.9 us (6%)
  local copies, waits for them, and re-layouts  12.1 us (5%)
  starting transfers between devices  5.39 us (2%)
    psum x1, waiting for transfers between devices, local(): lax.psum(lax.psum((remaining[:, None, None] * prompt_state, remaining[:,...  146 us
    psum x1, waiting for transfers between devices, local(): lax.psum((remaining[:, None, None] * prompt_state, remaining[:, None] * p...  20 us
    all_gather x1, blocking collectives, local(): totals = lax.all_gather(prompt_total, ('req', 'sp'))  13.4 us
    convert_element_type x1, other arithmetic, local(): (mixed * lax.rsqrt(meansq + 1e-05)[:, None] * norm_gain[None, :]).astype(...  8.57 us
    dot_general x1, matrix products, intra_block(): jnp.einsum('gqts,sgqp->tgqp', mixing, input_groups, preferred_element_typ...  6.32 us
    dot_general x2, matrix products, block_state(): jnp.einsum('tgqp,tgn->gqpn', scaled, rows_b, preferred_element_type=jnp.f...  5.66 us
    ppermute x2, starting transfers between devices, local(): lax.ppermute((block_total, local_state), 'sp', [(0, 1)])  5.35 us
  transfers between devices with their start and end apart: 4, of which 2 were waited for; matrix products, arithmetic and copies ran while one was open for 6% of the time, Pallas kernels for 0%

profile of v1, /device:TPU:0, one launch (start us, length us, event | category | flops | bytes accessed | tf_op | source)
XLA Modules:
  0.0 252.3 jit_solution(136720457371602978)
XLA Ops:
  6.5 0.7 neg.9
  7.2 0.8 broadcast_multiply_fusion
  8.0 0.1 reduce_window_sum.26
  8.1 0.8 exponential_multiply_fusion.1
  8.9 0.1 copy.45
  9.0 3.3 %copy.53 = f32[64,8192]{0,1:T(8,128)} copy(bf16[64,8192]{1,0:T(8,128)(2,1)} %param.13) | data formatting | bytes 3145728 | tf_op jit(solution)/shard_map/reshape | solution.py:19
  12.3 13.4 %all-gather = f32[8,1,128]{2,1,0:T(1,128)S(1)} all-gather(f32[1,1,128]{2,1,0:T(1,128)S(1)} %get-tuple-element.19), channel_id=1, replica_groups=mesh['parts'=2,'req'=4,'tp'=2,'sp'=2] {'req','sp'}, dimensions={0}, use_global_device_ids=true | all-gather | bytes 4608 | tf_op jit(solution)/shard_map/all_gather | solution.py:82
  25.8 0.2 fusion.32
  25.9 2.9 %fusion.16 = f32[4,32,64,128]{3,2,1,0:T(8,128)S(1)} fusion(f32[64,4,32,64]{0,3,2,1:T(8,128)} %bitcast.80, f32[64,4,32]{0,2,1:T(8,128)S(1)} %bitcast.85, bf16[64,4,128,1]{2,1,0,3:T(4,128)(2,1)S(1)} %bitcast.76), kind=kOutput, calls=%fused_computation.26 | convolution fusion | flops 135266304 | bytes 6389760 | tf_op jit(solution)/shard_map/tgqp,tgn->gqpn/dot_general | solution.py:22
  28.8 2.3 bitcast_multiply_fusion.1
  31.1 0.7 bitcast_multiply_fusion.3
  32.1 0.2 reduce_window_sum.24
  33.8 0.6 fusion.34
  34.4 0.1 select_reduce_fusion
  34.5 0.6 broadcast_multiply_fusion.1
  35.3 3.4 %copy.39 = bf16[1,128,8192]{1,2,0:T(8,128)(2,1)S(1)} copy(bf16[1,128,8192]{2,1,0:T(8,128)(2,1)} %param.16) | data formatting | bytes 4194304 | tf_op args[3]
  38.7 0.1 fusion.36
  38.8 0.1 fusion.37
  38.9 20.0 %all-reduce.7.cloned.1.call-done = (f32[128,64,128]{2,1,0:T(8,128)}, f32[128,128]{1,0:T(8,128)}) async-done(((f32[128,64,128]{2,1,0:T(8,128)}, f32[128,128]{1,0:T(8,128)}), (f32[128,64,128]{2,1,0:T(8,128)}, f32[128,128]{1,0:T(8,128)})) %all-reduce.7.cloned.1.call-update) | async-done | bytes 4259856 | tf_op jit(solution)/shard_map/psum | solution.py:86
  58.9 2.8 %fusion.17 = f32[4,32,64,128]{3,2,1,0:T(8,128)} fusion(f32[128,4,32]{0,2,1:T(8,128)S(1)} %get-tuple-element.16, bf16[1,128,1,4,128]{4,3,2,1,0:T(4,128)(2,1)S(1)} %get-tuple-element.10, f32[4,32,64]{2,1,0:T(8,128)S(1)} %mul.204, bf16[128,4,32,64]{0,3,2,1:T(8,128)(2,1)S(1)} %bitcast.77), kind=kOutput, calls=%fused_computation.27 | convolution fusion | flops 274726912 | bytes 6520832 | tf_op jit(solution)/shard_map/tgqp,tgn->gqpn/dot_general | solution.py:22
  61.7 4.1 %collective-permute-start.1 = (f32[128,64,128]{2,1,0:T(8,128)}, f32[128,64,128]{2,1,0:T(8,128)}, u32[]{:S(2)}, u32[]{:S(2)}) collective-permute-start(f32[128,64,128]{2,1,0:T(8,128)} %bitcast.24), channel_id=1, source_target_pairs={{0,1},{2,3},{4,5},{6,7},{8,9},{10,11},{12,13},{14,15},{16,17},{18,... | collective-permute-start | bytes 12582920 | tf_op jit(solution)/shard_map/ppermute | solution.py:103
  65.8 1.3 collective-permute-start
  67.1 0.2 fusion.24
  67.3 6.3 %fusion.4 = f32[4,32,64,128]{3,2,1,0:T(8,128)} fusion(f32[4,32,128]{2,1,0:T(8,128)S(1)} %get-tuple-element.15, f32[4,32,128]{2,1,0:T(8,128)S(1)} %get-tuple-element.14, f32[4,128,128]{2,1,0:T(8,128)S(1)} %fusion.24, pred[128,128]{1,0:T(8,128)(4,1)S(1)} %iota_compare_fusion, f32[4,32,64]{2,1,0:T(8,128)S(1)} %mul.204, bf16[128,4,32,64]{0,3,2,1:T(8,128)(2,1)S(1)} %bitcast.78), kind=kOutput, calls=%fused_computation.7 | convolution fusion | flops 279969792 | bytes 6733824 | tf_op jit(solution)/shard_map/gqts,sgqp->tgqp/dot_general | solution.py:53
  73.8 0.1 copy.44
  74.1 145.9 %all-reduce.5.cloned.1.call-done = (f32[128,64,128]{2,1,0:T(8,128)}, f32[128,128]{1,0:T(8,128)}) async-done(((f32[128,64,128]{2,1,0:T(8,128)}, f32[128,128]{1,0:T(8,128)}), (f32[128,64,128]{2,1,0:T(8,128)}, f32[128,128]{1,0:T(8,128)})) %all-reduce.5.cloned.1.call-update) | async-done | bytes 4259856 | tf_op jit(solution)/shard_map/psum | solution.py:85
  220.0 4.4 %add_convert_fusion.1 = bf16[128,64,128]{2,1,0:T(8,128)(2,1)S(1)} fusion(f32[128,64,128]{2,1,0:T(8,128)} %collective-permute-done.1, f32[128,64,128]{2,1,0:T(8,128)} %get-tuple-element.5, f32[128,128]{1,0:T(8,128)} %get-tuple-element.6, f32[128,64]{1,0:T(8,128)S(1)} %mul.225, f32[128]{0:T(128)S(1)} %exp.43), kind=kLoop, calls=%fused_computation.18 | loop fusion | flops 5242880 | bytes 10584576 | tf_op jit(solution)/shard_map/convert_element_type | solution.py:110
  224.4 0.2 copy-done.1
  224.7 3.2 %fusion.3 = (f32[128]{0:T(128)S(1)}, f32[4,32,64,128]{3,2,1,0:T(8,128)}) fusion(f32[4,32,64,128]{3,2,1,0:T(8,128)S(1)} %copy-done.1, f32[4,32]{1,0:T(4,128)S(1)} %mul.242, f32[128,4,32]{0,2,1:T(8,128)S(1)} %get-tuple-element.13, bf16[4,32,64,128]{3,2,1,0:T(8,128)(2,1)S(1)} %bitcast.83, bf16[1,128,1,4,128]{4,3,2,1,0:T(4,128)(2,1)S(1)} %get-tuple-element.9, ...), kind=kOutput, calls=%fused_computation.6 | convolution fusion | flops 278921088 | bytes 12813312 | tf_op jit(solution)/shard_map/tgn,gqpn->tgqp/dot_general | solution.py:111
  227.9 4.9 %psum.39 = f32[128]{0:T(128)S(1)} all-reduce(f32[128]{0:T(128)S(1)} %get-tuple-element.21), channel_id=1, replica_groups=mesh['parts'=2,'req'=4,'tp'=2,'sp'=2] {'tp'}, use_global_device_ids=true, to_apply=%region_10.11 | all-reduce | flops 128 | bytes 1024 | tf_op jit(solution)/shard_map/psum | solution.py:121
  232.8 8.6 %fusion.10 = bf16[1,128,8192]{1,2,0:T(8,128)(2,1)} fusion(f32[1,128,8192]{1,2,0:T(8,128)} %bitcast.81, f32[1,128,8192]{1,2,0:T(8,128)} %bitcast.82, f32[8192]{0:T(1024)S(1)} %copy-done.5, f32[128]{0:T(128)S(1)} %add_rsqrt_fusion, f32[8192]{0:T(1024)S(1)} %broadcast_multiply_fusion.1, f32[8192]{0:T(1024)S(1)} %mul.237, f32[128,128]{0,1:T(8,128)S(1)} %copy.44, ...), kind=kLoop, calls=%fused_computation.16 | loop fusion | flops 11534336 | bytes 12747264 | tf_op jit(solution)/shard_map/convert_element_type | solution.py:123
  241.4 4.1 %copy.49 = bf16[1,128,8192]{2,1,0:T(8,128)(2,1)} copy(bf16[1,128,8192]{1,2,0:T(8,128)(2,1)} %fusion.10) | data formatting | bytes 4194304 | tf_op jit(solution)/shard_map/convert_element_type | solution.py:123
  (40 shorter events, 1.0 us)
Async XLA Ops:
  6.5 19.2 %copy-start = (bf16[64,4,128]{2,1,0:T(4,128)(2,1)S(1)}, bf16[64,4,128]{2,1,0:T(4,128)(2,1)}, u32[]{:S(2)}) copy-start(bf16[64,4,128]{2,1,0:T(4,128)(2,1)} %param.14) | copy-start | bytes 196612
  6.5 52.3 %all-reduce.7.cloned.1.call-start = ((), (), s32[]{:S(2)}) async-start(), calls=%async_computation.1 | async-start | bytes 8519680 | tf_op jit(solution)/shard_map/psum | solution.py:86
  31.1 0.8 copy-start.4
  31.1 2.6 %copy-start.7 = (f32[9]{0:T(128)S(1)}, f32[9]{0:T(128)}, u32[]{:S(2)}) copy-start(f32[9]{0:T(128)} %param.23) | copy-start | bytes 112
  31.1 3.3 %copy-start.2 = (f32[7,8192]{1,0:T(8,128)S(1)}, f32[7,8192]{1,0:T(8,128)}, u32[]{:S(2)}) copy-start(f32[7,8192]{1,0:T(8,128)} %param.22) | copy-start | bytes 688132
  31.8 6.8 %copy-start.3 = (bf16[1,128,2,4,128]{4,3,2,1,0:T(4,128)(2,1)S(1)}, bf16[1,128,2,4,128]{4,3,2,1,0:T(4,128)(2,1)}, u32[]{:S(2)}) copy-start(bf16[1,128,2,4,128]{4,3,2,1,0:T(4,128)(2,1)} %param.17) | copy-start | bytes 786436
  31.9 188.1 %all-reduce.5.cloned.1.call-start = ((), (), s32[]{:S(2)}) async-start(), calls=%async_computation | async-start | bytes 8519680 | tf_op jit(solution)/shard_map/psum | solution.py:85
  61.7 12.4 %collective-permute-start.1 = (f32[128,64,128]{2,1,0:T(8,128)}, f32[128,64,128]{2,1,0:T(8,128)}, u32[]{:S(2)}, u32[]{:S(2)}) collective-permute-start(f32[128,64,128]{2,1,0:T(8,128)} %bitcast.24), channel_id=1, source_target_pairs={{0,1},{2,3},{4,5},{6,7},{8,9},{10,11},{12,13},{14,15},{16,17},{18,... | collective-permute-start | bytes 12582920 | tf_op jit(solution)/shard_map/ppermute | solution.py:103
  65.8 8.3 %collective-permute-start = (f32[128]{0:T(128)S(1)}, f32[128]{0:T(128)S(1)}, u32[]{:S(2)}, u32[]{:S(2)}) collective-permute-start(f32[128]{0:T(128)S(1)} %get-tuple-element.17), channel_id=1, source_target_pairs={{0,1},{2,3},{4,5},{6,7},{8,9},{10,11},{12,13},{14,15},{16,17},{18,... | collective-permute-start | bytes 1544 | tf_op jit(solution)/shard_map/ppermute | solution.py:103
  67.3 6.4 %copy-start.6 = (f32[128]{0:T(128)S(1)}, f32[128]{0:T(128)}, u32[]{:S(2)}) copy-start(f32[128]{0:T(128)} %param.20) | copy-start | bytes 1540
  220.0 4.7 %copy-start.1 = (f32[4,32,64,128]{3,2,1,0:T(8,128)S(1)}, f32[4,32,64,128]{3,2,1,0:T(8,128)}, u32[]{:S(2)}) copy-start(f32[4,32,64,128]{3,2,1,0:T(8,128)} %fusion.4) | copy-start | bytes 12582916
  224.7 8.2 %copy-start.5 = (f32[8192]{0:T(1024)S(1)}, f32[8192]{0:T(1024)}, u32[]{:S(2)}) copy-start(f32[8192]{0:T(1024)} %param.21) | copy-start | bytes 98308
Sparse Core Ops, SparseCore 0:
  32.0 26.8 all-reduce.6
  61.3 158.6 all-reduce.4
